TPU v7x, 256 devices: a whole 4x4x8 slice. The times are simulated.
256 devices in a mesh: re: 8 (over x, y_lo), rp: 16 (over z, core), mode: 2 (over y_hi).
Axes of the slice: x: 4, y: 4 (y_hi: 2, y_lo: 2; y = y_hi * 2 + y_lo), z: 8, core: 2. Of those that a mesh axis runs over, the one named last changes fastest.
Arguments:
- coupling: float32 [2, 64, 16, 120, 576], P(None, 're', 'rp', 'mode'), may hold values from -0.1875 to 0.1875
- electron_cells: int32 [64, 3], replicated, may hold values from -6 to 6
- phonon_cells: int32 [16, 3], replicated, may hold values from -3 to 3
- kpoint_index: int32 [16, 3], replicated, may hold values from 0 to 15
- qpoint_index: int32 [16, 3], replicated, may hold values from 0 to 15
- eigenvectors: float32 [16, 2, 120, 120], P('rp', None, 'mode'), may hold values from -0.5 to 0.5
- frequencies: float32 [16, 120], P('rp', 'mode'), may hold values from 0.25 to 2
Outputs:
- mode_coupling: float32 [120, 16, 16, 2, 576], P('mode', 'rp', 're')
All inputs are finite; a program needn't handle non-finite values.
Results may differ from a plain program's by a relative error of at most 0.00007.
Values sent between devices are 32-bit elements; how exact they have to be, the bound alone decides.
No kernel may reach another device: no remote copies, remote signals or barrier semaphores. Data moves between devices by JAX's collectives and lax.ppermute only.
A program may use at most 64 MiB of HBM per device.

v0:
```python
import functools

import jax
import jax.numpy as jnp
from jax import lax
from jax.experimental import pallas as pl
from jax.experimental.pallas import tpu as pltpu
from jax.sharding import PartitionSpec as P


KG = 16
LANES = 128
HALF = 64


def exchange(parts, axis):
    return lax.all_to_all(parts, axis, split_axis=0, concat_axis=0, tiled=True)


def split(x):
    high = x.astype(jnp.bfloat16)
    return high, (x - high.astype(jnp.float32)).astype(jnp.bfloat16)


def dot(a, b):
    return jnp.dot(a, b, preferred_element_type=jnp.float32)


def phases(points_ref, cells_ref, stride=1):
    points = points_ref[...].astype(jnp.float32)
    count = points.shape[1]
    if stride > 1:
        old = lax.broadcasted_iota(jnp.int32, (count, count), 0)
        new = lax.broadcasted_iota(jnp.int32, (count, count), 1)
        at = old % stride * (count // stride) + old // stride
        points = jnp.dot(
            points, jnp.where(at == new, 1.0, 0.0), precision=lax.Precision.HIGHEST
        )
    exact = lax.dot_general(
        points,
        cells_ref[...].astype(jnp.float32),
        (((0,), (0,)), ((), ())),
        precision=lax.Precision.HIGHEST,
        preferred_element_type=jnp.float32,
    )
    turns = exact.astype(jnp.int32) & (KG - 1)
    angle = turns.astype(jnp.float32) * (2.0 * 3.141592653589793 / KG)
    high, low = split(jnp.concatenate([jnp.cos(angle), jnp.sin(angle)], axis=0))
    return jnp.concatenate([high, high, low], axis=1)


def turn(table, block, count):
    high, low = split(block)
    both = dot(table, jnp.concatenate([high, low, high], axis=0))
    parts = []
    for at in range(0, block.shape[1], LANES):
        cos_part = both[:count, at : at + LANES]
        sin_part = pltpu.roll(both[count:, at : at + LANES], HALF, 1)
        lane = lax.broadcasted_iota(jnp.int32, sin_part.shape, 1)
        parts.append(cos_part + jnp.where(lane < HALF, -sin_part, sin_part))
    return parts


def lay_out(x_ref, *refs, kk):
    o_ref, e_ref, p_ref, buf, held, sems, small_sems = refs[4:11]
    _, nr, modes, _, pairs = x_ref.shape
    small = [
        pltpu.make_async_copy(refs[i], refs[11 + i], small_sems.at[i]) for i in range(4)
    ]
    copies = [
        pltpu.make_async_copy(x_ref.at[:, r], buf.at[r], sems.at[r]) for r in range(nr)
    ]
    for copy in copies[:1] + small + copies[1:]:
        copy.start()
    held[...] = jnp.zeros_like(held)
    for r in range(nr):
        copies[r].wait()
        if r == nr // 2:
            for copy in small:
                copy.wait()
            e_ref[...] = phases(refs[11], refs[12], kk)
            p_ref[...] = phases(refs[13], refs[14])
        slot = r % 2
        held[slot, :modes] = buf[r, 0, :, 0, :]
        held[slot, HALF : HALF + modes] = buf[r, 1, :, 0, :]
        o_ref[pl.ds(r, pairs, stride=nr), :] = held[slot].T


def electron(t_ref, x_ref, o_ref):
    src, points = x_ref.shape[:2]
    nk = t_ref.shape[0] // 2
    table = t_ref[...]
    group = 8
    for start in range(0, points, group):
        cols = []
        for p in range(start, start + group):
            cols.append(jnp.concatenate([x_ref[i, p] for i in range(src)], axis=0))
        parts = turn(table, jnp.concatenate(cols, axis=1), nk)
        for t in range(group):
            o_ref[pl.ds(start + t, nk, stride=points), :] = parts[t]


def phonon(t_ref, x_ref, o_ref):
    nq, ns = t_ref.shape[0] // 2, t_ref.shape[1] // 3
    rows = x_ref.shape[0] // ns
    table = t_ref[...]
    group = 8
    for start in range(0, rows, group):
        cols = [x_ref[pl.ds(start + t, ns, stride=rows), :] for t in range(group)]
        parts = turn(table, jnp.concatenate(cols, axis=1), nq)
        for t in range(group):
            o_ref[pl.ds(start + t, nq, stride=rows), :] = parts[t]


def modes_of(x_ref, w_ref, o_ref, *, nk, pts, kk):
    owners = nk // kk
    w_high, w_low = split(w_ref[...])
    group = 9
    for start in range(0, pts, group):
        rows = []
        for p in range(start, start + group):
            both = [x_ref[pl.ds(m * pts + p, nk, stride=2 * pts), :] for m in range(2)]
            rows.append(jnp.concatenate(both, axis=1))
        high, low = split(jnp.concatenate(rows, axis=0))
        res = dot(high, w_high) + (dot(high, w_low) + dot(low, w_high))
        for t in range(group):
            for k in range(kk):
                at = t * nk + k * owners
                for m in range(2):
                    base = m * owners * pts * kk + (start + t) * kk + k
                    o_ref[pl.ds(base, owners, stride=pts * kk), :] = res[
                        at : at + owners, m * LANES : (m + 1) * LANES
                    ]


def finish(x_ref, o_ref, *, kk, pts):
    modes = o_ref.shape[0]
    owners = x_ref.shape[0] // (2 * kk * pts)
    for k in range(kk):
        rows = []
        for i in range(owners):
            for m in range(2):
                at = (m * owners + i) * pts * kk + k
                rows.append(x_ref[pl.ds(at, pts, stride=kk), :])
        turned = jnp.concatenate(rows, axis=0).T
        o_ref[:, 0, k, 0, :] = turned[:modes]
        o_ref[:, 0, k, 1, :] = turned[HALF : HALF + modes]


FAR = pl.BlockSpec(memory_space=pltpu.HBM)
WHOLE = pl.BlockSpec(memory_space=pltpu.VMEM)
ROOM = pltpu.CompilerParams(vmem_limit_bytes=20 * 2**20)


def far(x):
    return pltpu.with_memory_space_constraint(x, pltpu.HBM)


def near(x):
    return pltpu.with_memory_space_constraint(x, pltpu.VMEM)


def call(body, rows, *args):
    return pl.pallas_call(
        body,
        out_shape=pltpu.VMEM((rows, LANES), jnp.float32),
        in_specs=[WHOLE] * len(args),
        out_specs=WHOLE,
        compiler_params=ROOM,
    )(*args)


def shards(
    coupling, electron_cells, phonon_cells, kpoint_index, qpoint_index, eigenvectors, frequencies
):
    re_size = lax.axis_size("re")
    rp_size = lax.axis_size("rp")
    _, nr, _, modes, pairs = coupling.shape
    nk = kpoint_index.shape[0]
    nq = qpoint_index.shape[0]
    ns = phonon_cells.shape[0]
    peers = re_size * 2
    pts = pairs // peers
    kk = nk // re_size

    tables = [x.T for x in (kpoint_index, electron_cells, qpoint_index, phonon_cells)]
    laid, table_e, table_p = pl.pallas_call(
        functools.partial(lay_out, kk=kk),
        out_shape=[
            pltpu.VMEM((pairs * nr, LANES), jnp.float32),
            pltpu.VMEM((2 * nk, 3 * re_size * nr), jnp.bfloat16),
            pltpu.VMEM((2 * nq, 3 * ns), jnp.bfloat16),
        ],
        in_specs=[FAR] * 5,
        out_specs=[WHOLE] * 3,
        compiler_params=ROOM,
        scratch_shapes=[
            pltpu.VMEM((nr, 2, modes, 1, pairs), jnp.float32),
            pltpu.VMEM((2, LANES, pairs), jnp.float32),
            pltpu.SemaphoreType.DMA((nr,)),
            pltpu.SemaphoreType.DMA((4,)),
        ]
        + [pltpu.VMEM(x.shape, x.dtype) for x in tables],
    )(far(coupling.transpose(0, 1, 3, 2, 4)), *[far(x) for x in tables])
    got = exchange(laid.reshape(re_size, 2 * pts * nr, LANES), "re")
    bloch_k = call(
        electron,
        nk * pts * 2,
        table_e,
        near(got.reshape(re_size, 2 * pts, nr, LANES)),
    )

    got = exchange(bloch_k.reshape(rp_size, pts * 2, LANES), "rp")
    bloch_kq = call(
        phonon,
        nq * pts * 2,
        table_p,
        near(got.reshape(ns * pts * 2, LANES)),
    )

    bloch_kq, eigenvectors, frequencies = lax.optimization_barrier(
        (bloch_kq, eigenvectors, frequencies)
    )
    packed = jnp.concatenate(
        [eigenvectors[0].reshape(2 * modes, -1), jnp.pad(frequencies, ((0, 0), (0, modes)))]
    )
    other = lax.ppermute(packed, "mode", [(0, 1), (1, 0)])
    both = jnp.stack([packed, other])
    both = jnp.where(lax.axis_index("mode") == 0, both, both[::-1])
    scale = lax.rsqrt(2.0 * both[:, -1, :modes]).reshape(-1)
    vec = both[:, :-1].reshape(2, 2, modes, 2 * modes) * scale
    real = jnp.stack([vec[:, 0], -vec[:, 1]], axis=1)
    imag = jnp.stack([vec[:, 1], vec[:, 0]], axis=1)
    weight = jnp.stack([real, imag], axis=3)
    weight = weight.reshape(2, 2, modes, 2, 2, modes).transpose(0, 1, 2, 4, 3, 5)
    gap = HALF - modes
    weight = jnp.pad(weight, ((0, 0), (0, 0), (0, gap), (0, 0), (0, 0), (0, gap)))
    weight = weight.reshape(2 * LANES, 2 * LANES)

    got = exchange(bloch_kq.reshape(rp_size * 2, pts // 4, 4, LANES), ("rp", "mode"))
    rotated = call(
        functools.partial(modes_of, nk=nk, pts=pts, kk=kk),
        peers * pts * kk,
        near(got.reshape(nk * pts * 2, LANES)),
        weight,
    )

    got = exchange(rotated.reshape(peers, pts * kk, LANES), ("mode", "re"))
    return pl.pallas_call(
        functools.partial(finish, kk=kk, pts=pts),
        out_shape=jax.ShapeDtypeStruct((modes, 1, kk, 2, pairs), jnp.float32),
        in_specs=[WHOLE],
        out_specs=WHOLE,
        compiler_params=ROOM,
    )(near(got.reshape(pairs * kk, LANES)))


def solution(mesh):
    placed = (
        P(None, "re", "rp", "mode", None),
        P(),
        P(),
        P(),
        P(),
        P("rp", None, "mode", None),
        P("rp", "mode"),
    )
    return jax.shard_map(
        shards,
        mesh=mesh,
        in_specs=placed,
        out_specs=P("mode", "rp", "re", None, None),
        check_vma=False,
    )
```

profile of v0, /device:TPU:1, one launch (start us, length us, event | category | flops | bytes accessed | tf_op | source)
XLA Modules:
  0.0 111.2 jit_solution(13572788431023675111)
XLA Ops:
  0.0 2.8 %shard_map.73 = (f32[4608,128]{1,0:T(8,128)S(1)}, bf16[32,192]{1,0:T(8,128)(2,1)S(1)}, bf16[32,48]{1,0:T(8,128)(2,1)S(1)}) custom-call(f32[2,8,60,1,576]{4,3,2,1,0:T(1,128)} %bitcast.30, s32[3,16]{1,0:T(4,128)} %bitcast.33, s32[3,64]{1,0:T(4,128)} %bitcast.34, s32[3,16]{1,0:T(4,128)} %bitcast.35, s32[3,16]{1,0:T(4,128)} %bitcast.36), custom_call_target="tpu_custom_call" | custom-call | tf_op jit(solution)/shard_map/pallas_call | solution.py:187
  2.8 34.3 %all_to_all.20 = f32[8,576,128]{2,1,0:T(8,128)S(1)} all-to-all(f32[8,576,128]{2,1,0:T(8,128)S(1)} %bitcast.24), channel_id=1, replica_groups=mesh['re'=8,'rp'=16,'mode'=2] {'re'}, dimensions={0} | all-to-all | bytes 4718592 | tf_op jit(solution)/shard_map/all_to_all | solution.py:17
  37.1 0.0 copy-start
  37.1 0.0 copy-start.1
  37.1 0.8 shard_map.74
  38.0 29.0 %all_to_all.21 = f32[16,72,128]{2,1,0:T(8,128)S(1)} all-to-all(f32[16,72,128]{2,1,0:T(8,128)S(1)} %bitcast.29), channel_id=1, replica_groups=mesh['re'=8,'rp'=16,'mode'=2] {'rp'}, dimensions={0} | all-to-all | bytes 1179648 | tf_op jit(solution)/shard_map/all_to_all | solution.py:17
  67.0 1.2 %shard_map.75 = f32[1152,128]{1,0:T(8,128)} custom-call(bf16[32,48]{1,0:T(8,128)(2,1)S(1)} %get-tuple-element.11.t_ref, f32[1152,128]{1,0:T(8,128)S(1)} %bitcast.26), custom_call_target="tpu_custom_call" | custom-call | tf_op jit(solution)/shard_map/pallas_call | solution.py:164
  68.2 0.0 copy-done
  68.2 0.0 copy-done.1
  68.2 2.7 %collective-permute-start = (f32[121,120]{1,0:T(8,128)S(1)}, f32[121,120]{1,0:T(8,128)S(1)}, u32[]{:S(2)}, u32[]{:S(2)}) collective-permute-start(f32[121,120]{1,0:T(8,128)S(1)} %get-tuple-element.21), channel_id=1, source_target_pairs={{0,1},{1,0},{2,3},{3,2},{4,5},{5,4},{6,7},{7,6},{8,9},{9,8},{10,11... | collective-permute-start | bytes 174248 | tf_op jit(solution)/shard_map/ppermute | solution.py:227
  71.0 3.9 %all-to-all-start.2 = ((f32[32,9,4,128]{3,2,1,0:T(4,128)}), f32[32,9,4,128]{3,2,1,0:T(4,128)S(1)}, u32[]{:S(2)}, u32[]{:S(2)}) async-start(f32[32,9,4,128]{3,2,1,0:T(4,128)} %bitcast.9), calls=%async_computation.2 | async-start | bytes 1179648 | tf_op jit(solution)/shard_map/all_to_all | solution.py:17
  74.9 0.0 collective-permute-done
  75.0 0.1 copy.19
  75.1 0.1 rsqrt.11
  75.3 0.1 pad_maximum_fusion.1
  75.4 0.1 copy.21
  75.5 0.2 stack.31
  75.7 0.1 copy.20
  75.8 0.2 stack.29
  76.0 0.3 maximum_bitcast_fusion
  76.3 0.4 copy.24
  76.6 0.2 pad.9.clone
  76.8 0.5 reshape.51.w_ref
  77.3 15.7 %all-to-all-done.2 = f32[32,9,4,128]{3,2,1,0:T(4,128)S(1)} async-done(((f32[32,9,4,128]{3,2,1,0:T(4,128)}), f32[32,9,4,128]{3,2,1,0:T(4,128)S(1)}, u32[]{:S(2)}, u32[]{:S(2)}) %all-to-all-start.2) | async-done | bytes 589856 | tf_op jit(solution)/shard_map/all_to_all | solution.py:17
  93.0 0.4 shard_map.76
  93.4 16.7 %all_to_all.22 = f32[16,72,128]{2,1,0:T(8,128)S(1)} all-to-all(f32[16,72,128]{2,1,0:T(8,128)S(1)} %bitcast.27), channel_id=1, replica_groups=mesh['re'=8,'rp'=16,'mode'=2] {'mode','re'}, dimensions={0} | all-to-all | bytes 1179648 | tf_op jit(solution)/shard_map/all_to_all | solution.py:17
  110.1 1.1 shard_map.77
  (9 shorter events, 0.2 us)
Async XLA Ops:
  37.1 31.1 %copy-start = (f32[1,2,60,120]{3,1,2,0:T(2,128)S(1)}, f32[1,2,60,120]{3,1,2,0:T(2,128)}, u32[]{:S(2)}) copy-start(f32[1,2,60,120]{3,1,2,0:T(2,128)} %param.12) | copy-start | bytes 172804
  37.1 31.1 %copy-start.1 = (f32[1,60]{1,0:T(1,128)S(1)}, f32[1,60]{1,0:T(1,128)}, u32[]{:S(2)}) copy-start(f32[1,60]{1,0:T(1,128)} %param.13) | copy-start | bytes 724
  68.2 6.7 %collective-permute-start = (f32[121,120]{1,0:T(8,128)S(1)}, f32[121,120]{1,0:T(8,128)S(1)}, u32[]{:S(2)}, u32[]{:S(2)}) collective-permute-start(f32[121,120]{1,0:T(8,128)S(1)} %get-tuple-element.21), channel_id=1, source_target_pairs={{0,1},{1,0},{2,3},{3,2},{4,5},{5,4},{6,7},{7,6},{8,9},{9,8},{10,11... | collective-permute-start | bytes 174248 | tf_op jit(solution)/shard_map/ppermute | solution.py:227
  71.0 22.1 %all-to-all-start.2 = ((f32[32,9,4,128]{3,2,1,0:T(4,128)}), f32[32,9,4,128]{3,2,1,0:T(4,128)S(1)}, u32[]{:S(2)}, u32[]{:S(2)}) async-start(f32[32,9,4,128]{3,2,1,0:T(4,128)} %bitcast.9), calls=%async_computation.2 | async-start | bytes 1179648 | tf_op jit(solution)/shard_map/all_to_all | solution.py:17
where the time goes:
time: 112 us; the launch traced here: 111 us
  blocking collectives  80 us (71%)
  waiting for transfers between devices  15.7 us (14%)
  starting transfers between devices  6.66 us (6%)
  Pallas kernels  6.4 us (6%)
  local copies, waits for them, and re-layouts  1.78 us (2%)
    all_to_all x3, blocking collectives, exchange(): return lax.all_to_all(parts, axis, split_axis=0, concat_axis=0, tiled=True)  80 us
    all_to_all x1, waiting for transfers between devices, exchange(): return lax.all_to_all(parts, axis, split_axis=0, concat_axis=0, tiled=True)  15.7 us
    all_to_all x1, starting transfers between devices, exchange(): return lax.all_to_all(parts, axis, split_axis=0, concat_axis=0, tiled=True)  3.95 us
    pallas_call x1, Pallas kernels, shards(): pl.pallas_call(functools.partial(lay_out, kk=kk), out_shape=[pltpu.VMEM((...  2.84 us
    ppermute x1, starting transfers between devices, shards(): other = lax.ppermute(packed, 'mode', [(0, 1), (1, 0)])  2.71 us
    pallas_call x3, Pallas kernels, call(): pl.pallas_call(body, out_shape=pltpu.VMEM((rows, LANES), jnp.float32), in...  2.45 us
  transfers between devices with their start and end apart: 2, of which 1 were waited for; matrix products, arithmetic and copies ran while one was open for 2% of the time, Pallas kernels for 0%

commit v1 on v0

--- a/solution.py
+++ b/solution.py
@@ -109,7 +109,8 @@
         cols = [x_ref[pl.ds(start + t, ns, stride=rows), :] for t in range(group)]
         parts = turn(table, jnp.concatenate(cols, axis=1), nq)
         for t in range(group):
-            o_ref[pl.ds(start + t, nq, stride=rows), :] = parts[t]
+            half, p = divmod(start + t, rows // 2)
+            o_ref[pl.ds(half * nq * (rows // 2) + p, nq, stride=rows // 2), :] = parts[t]
 
 
 def modes_of(x_ref, w_ref, o_ref, *, nk, pts, kk):
@@ -119,7 +120,7 @@
     for start in range(0, pts, group):
         rows = []
         for p in range(start, start + group):
-            both = [x_ref[pl.ds(m * pts + p, nk, stride=2 * pts), :] for m in range(2)]
+            both = [x_ref[pl.ds(m * nk * pts + p, nk, stride=pts), :] for m in range(2)]
             rows.append(jnp.concatenate(both, axis=1))
         high, low = split(jnp.concatenate(rows, axis=0))
         res = dot(high, w_high) + (dot(high, w_low) + dot(low, w_high))
@@ -237,7 +238,7 @@
     weight = jnp.pad(weight, ((0, 0), (0, 0), (0, gap), (0, 0), (0, 0), (0, gap)))
     weight = weight.reshape(2 * LANES, 2 * LANES)
 
-    got = exchange(bloch_kq.reshape(rp_size * 2, pts // 4, 4, LANES), ("rp", "mode"))
+    got = exchange(bloch_kq.reshape(rp_size * 2, pts // 4, 4, LANES), ("mode", "rp"))
     rotated = call(
         functools.partial(modes_of, nk=nk, pts=pts, kk=kk),
         peers * pts * kk,

time: 112 us -> 110 us (0.982)
  blocking collectives: 80 us -> 76.3 us
  waiting for transfers between devices: 15.7 us -> 17 us
    all_to_all x3, blocking collectives: 80 us -> 76.3 us  [exchange(): return lax.all_to_all(parts, axis, split_axis=0, concat_axis=0, tiled=True)]
    all_to_all x1, waiting for transfers between devices: 15.7 us -> 17 us  [exchange(): return lax.all_to_all(parts, axis, split_axis=0, concat_axis=0, tiled=True)]
where the time goes in v1:
time: 110 us; the launch traced here: 109 us
  blocking collectives  76.3 us (69%)
  waiting for transfers between devices  17 us (15%)
  starting transfers between devices  6.65 us (6%)
  Pallas kernels  6.38 us (6%)
  local copies, waits for them, and re-layouts  1.78 us (2%)
    all_to_all x3, blocking collectives, exchange(): return lax.all_to_all(parts, axis, split_axis=0, concat_axis=0, tiled=True)  76.3 us
    all_to_all x1, waiting for transfers between devices, exchange(): return lax.all_to_all(parts, axis, split_axis=0, concat_axis=0, tiled=True)  17 us
    all_to_all x1, starting transfers between devices, exchange(): return lax.all_to_all(parts, axis, split_axis=0, concat_axis=0, tiled=True)  3.94 us
    pallas_call x1, Pallas kernels, shards(): pl.pallas_call(functools.partial(lay_out, kk=kk), out_shape=[pltpu.VMEM((...  2.84 us
    ppermute x1, starting transfers between devices, shards(): other = lax.ppermute(packed, 'mode', [(0, 1), (1, 0)])  2.71 us
    pallas_call x3, Pallas kernels, call(): pl.pallas_call(body, out_shape=pltpu.VMEM((rows, LANES), jnp.float32), in...  2.44 us
  transfers between devices with their start and end apart: 2, of which 1 were waited for; matrix products, arithmetic and copies ran while one was open for 2% of the time, Pallas kernels for 0%

profile of v1, /device:TPU:1, one launch (start us, length us, event | category | flops | bytes accessed | tf_op | source)
XLA Modules:
  0.0 108.8 jit_solution(7834462438299743154)
XLA Ops:
  0.0 2.8 %shard_map.73 = (f32[4608,128]{1,0:T(8,128)S(1)}, bf16[32,192]{1,0:T(8,128)(2,1)S(1)}, bf16[32,48]{1,0:T(8,128)(2,1)S(1)}) custom-call(f32[2,8,60,1,576]{4,3,2,1,0:T(1,128)} %bitcast.30, s32[3,16]{1,0:T(4,128)} %bitcast.33, s32[3,64]{1,0:T(4,128)} %bitcast.34, s32[3,16]{1,0:T(4,128)} %bitcast.35, s32[3,16]{1,0:T(4,128)} %bitcast.36), custom_call_target="tpu_custom_call" | custom-call | tf_op jit(solution)/shard_map/pallas_call | solution.py:188
  2.8 34.3 %all_to_all.20 = f32[8,576,128]{2,1,0:T(8,128)S(1)} all-to-all(f32[8,576,128]{2,1,0:T(8,128)S(1)} %bitcast.24), channel_id=1, replica_groups=mesh['re'=8,'rp'=16,'mode'=2] {'re'}, dimensions={0} | all-to-all | bytes 4718592 | tf_op jit(solution)/shard_map/all_to_all | solution.py:17
  37.1 0.0 copy-start
  37.1 0.0 copy-start.1
  37.1 0.8 shard_map.74
  38.0 29.0 %all_to_all.21 = f32[16,72,128]{2,1,0:T(8,128)S(1)} all-to-all(f32[16,72,128]{2,1,0:T(8,128)S(1)} %bitcast.29), channel_id=1, replica_groups=mesh['re'=8,'rp'=16,'mode'=2] {'rp'}, dimensions={0} | all-to-all | bytes 1179648 | tf_op jit(solution)/shard_map/all_to_all | solution.py:17
  67.0 1.2 %shard_map.75 = f32[1152,128]{1,0:T(8,128)} custom-call(bf16[32,48]{1,0:T(8,128)(2,1)S(1)} %get-tuple-element.11.t_ref, f32[1152,128]{1,0:T(8,128)S(1)} %bitcast.26), custom_call_target="tpu_custom_call" | custom-call | tf_op jit(solution)/shard_map/pallas_call | solution.py:165
  68.2 0.0 copy-done
  68.2 0.0 copy-done.1
  68.2 2.7 %collective-permute-start = (f32[121,120]{1,0:T(8,128)S(1)}, f32[121,120]{1,0:T(8,128)S(1)}, u32[]{:S(2)}, u32[]{:S(2)}) collective-permute-start(f32[121,120]{1,0:T(8,128)S(1)} %get-tuple-element.21), channel_id=1, source_target_pairs={{0,1},{1,0},{2,3},{3,2},{4,5},{5,4},{6,7},{7,6},{8,9},{9,8},{10,11... | collective-permute-start | bytes 174248 | tf_op jit(solution)/shard_map/ppermute | solution.py:228
  71.0 3.9 %all-to-all-start.2 = ((f32[32,9,4,128]{3,2,1,0:T(4,128)}), f32[32,9,4,128]{3,2,1,0:T(4,128)S(1)}, u32[]{:S(2)}, u32[]{:S(2)}) async-start(f32[32,9,4,128]{3,2,1,0:T(4,128)} %bitcast.9), calls=%async_computation.2 | async-start | bytes 1179648 | tf_op jit(solution)/shard_map/all_to_all | solution.py:17
  74.9 0.0 collective-permute-done
  75.0 0.1 copy.19
  75.1 0.1 rsqrt.11
  75.3 0.1 pad_maximum_fusion.1
  75.4 0.1 copy.21
  75.4 0.2 stack.31
  75.7 0.1 copy.20
  75.8 0.2 stack.29
  76.0 0.3 maximum_bitcast_fusion
  76.2 0.4 copy.24
  76.6 0.2 pad.9.clone
  76.8 0.5 reshape.51.w_ref
  77.3 17.0 %all-to-all-done.2 = f32[32,9,4,128]{3,2,1,0:T(4,128)S(1)} async-done(((f32[32,9,4,128]{3,2,1,0:T(4,128)}), f32[32,9,4,128]{3,2,1,0:T(4,128)S(1)}, u32[]{:S(2)}, u32[]{:S(2)}) %all-to-all-start.2) | async-done | bytes 589856 | tf_op jit(solution)/shard_map/all_to_all | solution.py:17
  94.3 0.4 shard_map.76
  94.7 13.0 %all_to_all.22 = f32[16,72,128]{2,1,0:T(8,128)S(1)} all-to-all(f32[16,72,128]{2,1,0:T(8,128)S(1)} %bitcast.27), channel_id=1, replica_groups=mesh['re'=8,'rp'=16,'mode'=2] {'mode','re'}, dimensions={0} | all-to-all | bytes 1179648 | tf_op jit(solution)/shard_map/all_to_all | solution.py:17
  107.7 1.1 %shard_map.77 = f32[60,1,2,2,576]{4,3,2,1,0:T(2,128)} custom-call(f32[1152,128]{1,0:T(8,128)S(1)} %bitcast.28), custom_call_target="tpu_custom_call" | custom-call | tf_op jit(solution)/shard_map/pallas_call | solution.py:250
  (9 shorter events, 0.2 us)
Async XLA Ops:
  37.1 31.1 %copy-start = (f32[1,2,60,120]{3,1,2,0:T(2,128)S(1)}, f32[1,2,60,120]{3,1,2,0:T(2,128)}, u32[]{:S(2)}) copy-start(f32[1,2,60,120]{3,1,2,0:T(2,128)} %param.12) | copy-start | bytes 172804
  37.1 31.1 %copy-start.1 = (f32[1,60]{1,0:T(1,128)S(1)}, f32[1,60]{1,0:T(1,128)}, u32[]{:S(2)}) copy-start(f32[1,60]{1,0:T(1,128)} %param.13) | copy-start | bytes 724
  68.2 6.7 %collective-permute-start = (f32[121,120]{1,0:T(8,128)S(1)}, f32[121,120]{1,0:T(8,128)S(1)}, u32[]{:S(2)}, u32[]{:S(2)}) collective-permute-start(f32[121,120]{1,0:T(8,128)S(1)} %get-tuple-element.21), channel_id=1, source_target_pairs={{0,1},{1,0},{2,3},{3,2},{4,5},{5,4},{6,7},{7,6},{8,9},{9,8},{10,11... | collective-permute-start | bytes 174248 | tf_op jit(solution)/shard_map/ppermute | solution.py:228
  71.0 23.3 %all-to-all-start.2 = ((f32[32,9,4,128]{3,2,1,0:T(4,128)}), f32[32,9,4,128]{3,2,1,0:T(4,128)S(1)}, u32[]{:S(2)}, u32[]{:S(2)}) async-start(f32[32,9,4,128]{3,2,1,0:T(4,128)} %bitcast.9), calls=%async_computation.2 | async-start | bytes 1179648 | tf_op jit(solution)/shard_map/all_to_all | solution.py:17
